TPU v7x, 32 devices: a whole 2x2x4 slice. The times are simulated.
32 devices in a mesh: sweep: 16 (over z, y, x), cols: 2 (over core).
Axes of the slice: x: 2, y: 2, z: 4, core: 2. Of those that a mesh axis runs over, the one named last changes fastest.
Arguments:
- rhs: bfloat16 [4, 16, 256, 1024], P(None, 'sweep', None, 'cols'), may hold values from -6 to 6
- blocks: bfloat16 [3, 16, 6, 256, 256], P(None, 'sweep', None, 'cols'), may hold values from -0.1875 to 0.1875
- diag_inv: bfloat16 [4, 16, 256, 256], P(None, 'sweep', 'cols'), as said below
- neighbours: int32 [3, 16, 6], P(None, 'sweep'), may hold values from -1 to 47, as said below
Outputs:
- samples: bfloat16 [4, 16, 256, 1024], P(None, 'sweep', None, 'cols')
Inputs may be any that keep to these rules, and one draw needn't show every extreme that they name: neighbours[b, p, k] belongs to block row (b + 1, p): -1 marks an unused slot; a used slot names block row b * 16 + p - o for some o with 0 <= o <= min(5, p), and the used slots of one block row name distinct rows. The last owner's block rows use all 6 slots. `diag_inv`: every block is lower triangular with a positive diagonal.
All inputs are finite; a program needn't handle non-finite values.
Results may differ from a plain program's by a relative error of at most 0.0095.
Values may be sent and summed in bfloat16 or wider, within the bound.
A program may use at most 64 MiB of HBM per device.

v0:
```python
import jax
import jax.numpy as jnp
from jax import lax
from jax.sharding import PartitionSpec as P

REACH = 5


def shifted(block, axis, distance):
    devices = range(lax.axis_size(axis))
    route = [(i - distance, i) for i in devices if i - distance in devices]
    return lax.ppermute(block, axis, route)


def slot_offsets(row_ids, level, owners, me):
    valid = row_ids >= 0
    offset = jnp.where(valid, me - (row_ids - level * owners), 0)
    return (valid, offset)


def forward_sums(blk, stacked, valid, offset):
    picked = jnp.take(stacked, offset, axis=0) * valid.astype(jnp.bfloat16)[:, None, None]
    return jnp.einsum("kab,kbc->ac", blk, picked, preferred_element_type=jnp.float32)


def backward_parts(blk, upper, valid, offset):
    terms = jnp.einsum("kba,bc->kac", blk, upper, preferred_element_type=jnp.float32)
    hits = (offset[None, :] == jnp.arange(REACH + 1, dtype=jnp.int32)[:, None]) & valid[None, :]
    return jnp.einsum(
        "ok,kac->oac", hits.astype(jnp.float32), terms, precision=lax.Precision.HIGHEST
    )


def on_device(rhs, blocks, diag_inv, neighbours):
    owners = lax.axis_size("sweep")
    me = lax.axis_index("sweep")
    levels = rhs.shape[0]
    blocks_all, diag_all = (
        lax.all_gather(blocks, "cols", axis=3, tiled=True),
        lax.all_gather(diag_inv, "cols", axis=2, tiled=True),
    )
    solved = [
        jnp.dot(diag_all[0, 0], rhs[0, 0], preferred_element_type=jnp.float32).astype(jnp.bfloat16)
    ]
    for level in range(1, levels):
        previous = solved[level - 1]
        nearby = [previous]
        for offset_by in range(1, REACH + 1):
            nearby.append(shifted(previous, "sweep", offset_by))
        stacked = jnp.stack(nearby)
        valid, offset = slot_offsets(neighbours[level - 1, 0], level - 1, owners, me)
        sums = forward_sums(blocks_all[level - 1, 0], stacked, valid, offset)
        residue = (rhs[level, 0].astype(jnp.float32) - sums).astype(jnp.bfloat16)
        solved.append(
            jnp.dot(diag_all[level, 0], residue, preferred_element_type=jnp.float32).astype(
                jnp.bfloat16
            )
        )
    top = levels - 1
    samples = [None] * levels
    samples[top] = jnp.einsum(
        "ba,bc->ac", diag_all[top, 0], solved[top], preferred_element_type=jnp.float32
    ).astype(jnp.bfloat16)
    for level in range(levels - 2, -1, -1):
        valid, offset = slot_offsets(neighbours[level, 0], level, owners, me)
        parts = backward_parts(blocks_all[level, 0], samples[level + 1], valid, offset)
        rounded = lax.optimization_barrier(parts.astype(jnp.bfloat16))
        back_terms = rounded[0].astype(jnp.float32)
        for offset_by in range(1, REACH + 1):
            back_terms = back_terms + shifted(rounded[offset_by], "sweep", -offset_by).astype(
                jnp.float32
            )
        adjusted = (solved[level].astype(jnp.float32) - back_terms).astype(jnp.bfloat16)
        samples[level] = jnp.einsum(
            "ba,bc->ac", diag_all[level, 0], adjusted, preferred_element_type=jnp.float32
        ).astype(jnp.bfloat16)
    return jnp.stack(samples)[:, None]


def solution(mesh):
    placed = (
        P(None, "sweep", None, "cols"),
        P(None, "sweep", None, "cols", None),
        P(None, "sweep", "cols", None),
        P(None, "sweep", None),
    )
    return jax.shard_map(
        on_device,
        mesh=mesh,
        in_specs=placed,
        out_specs=P(None, "sweep", None, "cols"),
        check_vma=False,
    )
```

profile of v0, /device:TPU:12, one launch (start us, length us, event | category | flops | bytes accessed | tf_op | source)
XLA Modules:
  0.0 294.7 jit_solution(7072926268788419169)
XLA Ops:
  11.0 3.5 %collective-permute-start.3 = (bf16[256,512]{1,0:T(8,128)(2,1)S(1)}, bf16[256,512]{1,0:T(8,128)(2,1)S(1)}, u32[]{:S(2)}, u32[]{:S(2)}) collective-permute-start(bf16[256,512]{1,0:T(8,128)(2,1)S(1)} %get-tuple-element.38), channel_id=1, source_target_pairs={{0,8},{2,10},{4,12},{6,14},{8,16},{10,18},{12,20},{14,22},{16,24},... | collective-permute-start | bytes 786440 | tf_op jit(solution)/shard_map/ppermute | solution.py:12
  14.5 4.4 %collective-permute-start.2 = (bf16[256,512]{1,0:T(8,128)(2,1)S(1)}, bf16[256,512]{1,0:T(8,128)(2,1)S(1)}, u32[]{:S(2)}, u32[]{:S(2)}) collective-permute-start(bf16[256,512]{1,0:T(8,128)(2,1)S(1)} %get-tuple-element.38), channel_id=1, source_target_pairs={{0,6},{2,8},{4,10},{6,12},{8,14},{10,16},{12,18},{14,20},{16,22},{... | collective-permute-start | bytes 786440 | tf_op jit(solution)/shard_map/ppermute | solution.py:12
  18.9 3.4 %collective-permute-start.1 = (bf16[256,512]{1,0:T(8,128)(2,1)S(1)}, bf16[256,512]{1,0:T(8,128)(2,1)S(1)}, u32[]{:S(2)}, u32[]{:S(2)}) collective-permute-start(bf16[256,512]{1,0:T(8,128)(2,1)S(1)} %get-tuple-element.38), channel_id=1, source_target_pairs={{0,4},{2,6},{4,8},{6,10},{8,12},{10,14},{12,16},{14,18},{16,20},{1... | collective-permute-start | bytes 786440 | tf_op jit(solution)/shard_map/ppermute | solution.py:12
  26.5 12.7 %collective-permute-done = bf16[256,512]{1,0:T(8,128)(2,1)} collective-permute-done((bf16[256,512]{1,0:T(8,128)(2,1)S(1)}, bf16[256,512]{1,0:T(8,128)(2,1)}, u32[]{:S(2)}, u32[]{:S(2)}) %collective-permute-start) | collective-permute-done | bytes 262176 | tf_op jit(solution)/shard_map/ppermute | solution.py:12
  42.1 3.3 %bitcast_dynamic-update-slice_fusion.1 = (bf16[6,256,512]{1,2,0:T(8,128)(2,1)}, bf16[512,256]{1,0:T(8,128)(2,1)S(1)}) fusion(bf16[4,1,256,256]{3,2,1,0:T(8,128)(2,1)S(1)} %all_gather.6, bf16[6,256,512]{2,1,0:T(8,128)(2,1)} %gather_fusion, pred[6]{0:T(512)(128)(4,1)S(1)} %get-tuple-element.35, bf16[6]{0:T(256)(128)(2,1)S(1)} %get-tuple-element.30, ...), kind=kOutput, calls=%fused_computation.92 | convolution fusion | flops 471859200 | bytes 3277824 | tf_op jit(solution)/shard_map/dot_general | solution.py:55
  45.5 11.6 %collective-permute-start.5 = (bf16[256,512]{0,1:T(8,128)(2,1)S(1)}, bf16[256,512]{0,1:T(8,128)(2,1)S(1)}, u32[]{:S(2)}, u32[]{:S(2)}) collective-permute-start(bf16[256,512]{0,1:T(8,128)(2,1)S(1)} %bitcast.268), channel_id=1, source_target_pairs={{0,2},{2,4},{4,6},{6,8},{8,10},{10,12},{12,14},{14,16},{16,18},{18... | collective-permute-start | bytes 786440 | tf_op jit(solution)/shard_map/ppermute | solution.py:12
  59.0 8.5 %collective-permute-start.7 = (bf16[256,512]{0,1:T(8,128)(2,1)S(1)}, bf16[256,512]{0,1:T(8,128)(2,1)S(1)}, u32[]{:S(2)}, u32[]{:S(2)}) collective-permute-start(bf16[256,512]{0,1:T(8,128)(2,1)S(1)} %bitcast.270), channel_id=1, source_target_pairs={{0,6},{2,8},{4,10},{6,12},{8,14},{10,16},{12,18},{14,20},{16,22},{... | collective-permute-start | bytes 786440 | tf_op jit(solution)/shard_map/ppermute | solution.py:12
  75.0 9.2 %collective-permute-done.8 = bf16[256,512]{0,1:T(8,128)(2,1)S(1)} collective-permute-done((bf16[256,512]{0,1:T(8,128)(2,1)S(1)}, bf16[256,512]{0,1:T(8,128)(2,1)S(1)}, u32[]{:S(2)}, u32[]{:S(2)}) %collective-permute-start.8) | collective-permute-done | bytes 262176 | tf_op jit(solution)/shard_map/ppermute | solution.py:12
  85.7 3.4 %gather_fusion.1 = bf16[6,256,512]{1,2,0:T(8,128)(2,1)} fusion(bf16[6,256,512]{1,2,0:T(8,128)(2,1)} %bitcast_dynamic-update-slice_fusion.7, s32[1024]{0:T(1024)S(1)} %pad_clamp_fusion.1), kind=kCustom, calls=%fused_computation.1.clone | custom fusion | bytes 3145752 | tf_op jit(solution)/shard_map/jit(_take)/gather | solution.py:22
  89.1 3.1 %bitcast_dynamic-update-slice_fusion = (bf16[6,256,512]{1,2,0:T(8,128)(2,1)}, bf16[512,256]{1,0:T(8,128)(2,1)S(1)}) fusion(bf16[4,1,256,256]{3,2,1,0:T(8,128)(2,1)S(1)} %all_gather.6, bf16[6,256,512]{1,2,0:T(8,128)(2,1)} %gather_fusion.1, pred[6]{0:T(512)(128)(4,1)S(1)} %get-tuple-element.33, bf16[6]{0:T(256)(128)(2,1)S(1)} %get-tuple-element.29, ...), kind=kOutput, calls=%fused_computation.91 | convolution fusion | flops 471859200 | bytes 3277824 | tf_op jit(solution)/shard_map/dot_general | solution.py:55
  92.2 8.1 %collective-permute-start.10 = (bf16[256,512]{0,1:T(8,128)(2,1)S(1)}, bf16[256,512]{0,1:T(8,128)(2,1)S(1)}, u32[]{:S(2)}, u32[]{:S(2)}) collective-permute-start(bf16[256,512]{0,1:T(8,128)(2,1)S(1)} %bitcast.273), channel_id=1, source_target_pairs={{0,2},{2,4},{4,6},{6,8},{8,10},{10,12},{12,14},{14,16},{16,18},{18... | collective-permute-start | bytes 786440 | tf_op jit(solution)/shard_map/ppermute | solution.py:12
  102.3 5.3 %collective-permute-start.12 = (bf16[256,512]{0,1:T(8,128)(2,1)S(1)}, bf16[256,512]{0,1:T(8,128)(2,1)S(1)}, u32[]{:S(2)}, u32[]{:S(2)}) collective-permute-start(bf16[256,512]{0,1:T(8,128)(2,1)S(1)} %bitcast.275), channel_id=1, source_target_pairs={{0,6},{2,8},{4,10},{6,12},{8,14},{10,16},{12,18},{14,20},{16,22},{... | collective-permute-start | bytes 786440 | tf_op jit(solution)/shard_map/ppermute | solution.py:12
  107.6 2.4 collective-permute-start.14
  113.3 3.2 %collective-permute-done.12 = bf16[256,512]{0,1:T(8,128)(2,1)S(1)} collective-permute-done((bf16[256,512]{0,1:T(8,128)(2,1)S(1)}, bf16[256,512]{0,1:T(8,128)(2,1)S(1)}, u32[]{:S(2)}, u32[]{:S(2)}) %collective-permute-start.12) | collective-permute-done | bytes 262176 | tf_op jit(solution)/shard_map/ppermute | solution.py:12
  117.3 8.5 %collective-permute-done.13 = bf16[256,512]{0,1:T(8,128)(2,1)S(1)} collective-permute-done((bf16[256,512]{0,1:T(8,128)(2,1)S(1)}, bf16[256,512]{0,1:T(8,128)(2,1)S(1)}, u32[]{:S(2)}, u32[]{:S(2)}) %collective-permute-start.13) | collective-permute-done | bytes 262176 | tf_op jit(solution)/shard_map/ppermute | solution.py:12
  127.2 3.2 %gather_fusion.2 = bf16[6,256,512]{1,2,0:T(8,128)(2,1)} fusion(bf16[6,256,512]{1,2,0:T(8,128)(2,1)} %bitcast_dynamic-update-slice_fusion.2, s32[1024]{0:T(1024)S(1)} %pad_clamp_fusion), kind=kCustom, calls=%fused_computation.2.clone | custom fusion | bytes 3145752 | tf_op jit(solution)/shard_map/jit(_take)/gather | solution.py:22
  134.8 3.4 %copy.9 = f32[512,6,256]{0,1,2:T(8,128)} copy(f32[512,6,256]{2,0,1:T(8,128)S(1)} %fusion.34) | data formatting | bytes 6291456 | tf_op jit(solution)/shard_map/kba,bc->kac/dot_general | solution.py:27
  138.3 4.2 %fusion.4 = bf16[6,256,512]{2,0,1:T(8,128)(2,1)S(1)} fusion(f32[512,6,256]{0,1,2:T(8,128)} %copy.9, s32[6]{0:T(128)S(1)} %get-tuple-element.7, pred[6]{0:T(512)(128)(4,1)S(1)} %get-tuple-element.31), kind=kOutput, calls=%fused_computation.7 | convolution fusion | flops 56623176 | bytes 4718622 | tf_op jit(solution)/shard_map/ok,kac->oac/dot_general | solution.py:29
  142.5 2.5 copy.5
  156.3 11.6 %collective-permute-done.15 = bf16[256,512]{0,1:T(8,128)(2,1)S(1)} collective-permute-done((bf16[256,512]{0,1:T(8,128)(2,1)S(1)}, bf16[256,512]{0,1:T(8,128)(2,1)S(1)}, u32[]{:S(2)}, u32[]{:S(2)}) %collective-permute-start.15) | collective-permute-done | bytes 262176 | tf_op jit(solution)/shard_map/ppermute | solution.py:12
  167.9 23.4 %collective-permute-done.16 = bf16[256,512]{0,1:T(8,128)(2,1)S(1)} collective-permute-done((bf16[256,512]{0,1:T(8,128)(2,1)S(1)}, bf16[256,512]{0,1:T(8,128)(2,1)S(1)}, u32[]{:S(2)}, u32[]{:S(2)}) %collective-permute-start.16) | collective-permute-done | bytes 262176 | tf_op jit(solution)/shard_map/ppermute | solution.py:12
  194.3 3.4 %copy.10 = f32[512,6,256]{0,1,2:T(8,128)} copy(f32[512,6,256]{2,0,1:T(8,128)S(1)} %fusion.33) | data formatting | bytes 6291456 | tf_op jit(solution)/shard_map/kba,bc->kac/dot_general | solution.py:27
  197.8 4.2 %fusion.2 = bf16[6,256,512]{2,0,1:T(8,128)(2,1)S(1)} fusion(f32[512,6,256]{0,1,2:T(8,128)} %copy.10, s32[6]{0:T(128)S(1)} %get-tuple-element.34, pred[6]{0:T(512)(128)(4,1)S(1)} %get-tuple-element.32), kind=kOutput, calls=%fused_computation.5 | convolution fusion | flops 56623176 | bytes 4718622 | tf_op jit(solution)/shard_map/ok,kac->oac/dot_general | solution.py:29
  202.0 2.5 copy.6
  215.6 6.4 %collective-permute-done.20 = bf16[256,512]{0,1:T(8,128)(2,1)S(1)} collective-permute-done((bf16[256,512]{0,1:T(8,128)(2,1)S(1)}, bf16[256,512]{0,1:T(8,128)(2,1)S(1)}, u32[]{:S(2)}, u32[]{:S(2)}) %collective-permute-start.20) | collective-permute-done | bytes 262176 | tf_op jit(solution)/shard_map/ppermute | solution.py:12
  222.0 6.7 %collective-permute-done.22 = bf16[256,512]{0,1:T(8,128)(2,1)S(1)} collective-permute-done((bf16[256,512]{0,1:T(8,128)(2,1)S(1)}, bf16[256,512]{0,1:T(8,128)(2,1)S(1)}, u32[]{:S(2)}, u32[]{:S(2)}) %collective-permute-start.22) | collective-permute-done | bytes 262176 | tf_op jit(solution)/shard_map/ppermute | solution.py:12
  228.7 10.9 %collective-permute-done.21 = bf16[256,512]{0,1:T(8,128)(2,1)S(1)} collective-permute-done((bf16[256,512]{0,1:T(8,128)(2,1)S(1)}, bf16[256,512]{0,1:T(8,128)(2,1)S(1)}, u32[]{:S(2)}, u32[]{:S(2)}) %collective-permute-start.21) | collective-permute-done | bytes 262176 | tf_op jit(solution)/shard_map/ppermute | solution.py:12
  243.4 3.4 %copy.11 = f32[512,6,256]{0,1,2:T(8,128)} copy(f32[512,6,256]{2,0,1:T(8,128)S(1)} %fusion.32) | data formatting | bytes 6291456 | tf_op jit(solution)/shard_map/kba,bc->kac/dot_general | solution.py:27
  246.9 4.2 %fusion = bf16[6,256,512]{2,0,1:T(8,128)(2,1)S(1)} fusion(f32[512,6,256]{0,1,2:T(8,128)} %copy.11, s32[6]{0:T(128)S(1)} %get-tuple-element.36, pred[6]{0:T(512)(128)(4,1)S(1)} %get-tuple-element.27), kind=kOutput, calls=%fused_computation.3 | convolution fusion | flops 56623176 | bytes 4718622 | tf_op jit(solution)/shard_map/ok,kac->oac/dot_general | solution.py:29
  261.6 5.5 %collective-permute-done.25 = bf16[256,512]{1,0:T(8,128)(2,1)S(1)} collective-permute-done((bf16[256,512]{1,0:T(8,128)(2,1)S(1)}, bf16[256,512]{1,0:T(8,128)(2,1)S(1)}, u32[]{:S(2)}, u32[]{:S(2)}) %collective-permute-start.25) | collective-permute-done | bytes 262176 | tf_op jit(solution)/shard_map/ppermute | solution.py:12
  268.2 5.8 %collective-permute-done.27 = bf16[256,512]{1,0:T(8,128)(2,1)S(1)} collective-permute-done((bf16[256,512]{1,0:T(8,128)(2,1)S(1)}, bf16[256,512]{1,0:T(8,128)(2,1)S(1)}, u32[]{:S(2)}, u32[]{:S(2)}) %collective-permute-start.27) | collective-permute-done | bytes 262176 | tf_op jit(solution)/shard_map/ppermute | solution.py:12
  274.0 10.9 %collective-permute-done.26 = bf16[256,512]{1,0:T(8,128)(2,1)S(1)} collective-permute-done((bf16[256,512]{1,0:T(8,128)(2,1)S(1)}, bf16[256,512]{1,0:T(8,128)(2,1)S(1)}, u32[]{:S(2)}, u32[]{:S(2)}) %collective-permute-start.26) | collective-permute-done | bytes 262176 | tf_op jit(solution)/shard_map/ppermute | solution.py:12
  (109 shorter events, 77.6 us)
Async XLA Ops:
  6.5 35.6 %all-gather.2.cloned.1.call-start = ((), (), s32[]{:S(2)}) async-start(), calls=%async_computation | async-start | bytes 3538944 | tf_op jit(solution)/shard_map/all_gather | solution.py:39
  9.7 122.9 %copy-start.3 = (bf16[4,1,256,256]{3,2,1,0:T(8,128)(2,1)}, bf16[4,1,256,256]{3,2,1,0:T(8,128)(2,1)S(1)}, u32[]{:S(2)}) copy-start(bf16[4,1,256,256]{3,2,1,0:T(8,128)(2,1)S(1)} %all_gather.6) | copy-start | bytes 1572868
  11.0 29.2 %collective-permute-start.3 = (bf16[256,512]{1,0:T(8,128)(2,1)S(1)}, bf16[256,512]{1,0:T(8,128)(2,1)S(1)}, u32[]{:S(2)}, u32[]{:S(2)}) collective-permute-start(bf16[256,512]{1,0:T(8,128)(2,1)S(1)} %get-tuple-element.38), channel_id=1, source_target_pairs={{0,8},{2,10},{4,12},{6,14},{8,16},{10,18},{12,20},{14,22},{16,24},... | collective-permute-start | bytes 786440 | tf_op jit(solution)/shard_map/ppermute | solution.py:12
  14.5 25.7 %collective-permute-start.2 = (bf16[256,512]{1,0:T(8,128)(2,1)S(1)}, bf16[256,512]{1,0:T(8,128)(2,1)S(1)}, u32[]{:S(2)}, u32[]{:S(2)}) collective-permute-start(bf16[256,512]{1,0:T(8,128)(2,1)S(1)} %get-tuple-element.38), channel_id=1, source_target_pairs={{0,6},{2,8},{4,10},{6,12},{8,14},{10,16},{12,18},{14,20},{16,22},{... | collective-permute-start | bytes 786440 | tf_op jit(solution)/shard_map/ppermute | solution.py:12
  18.9 21.3 %collective-permute-start.1 = (bf16[256,512]{1,0:T(8,128)(2,1)S(1)}, bf16[256,512]{1,0:T(8,128)(2,1)S(1)}, u32[]{:S(2)}, u32[]{:S(2)}) collective-permute-start(bf16[256,512]{1,0:T(8,128)(2,1)S(1)} %get-tuple-element.38), channel_id=1, source_target_pairs={{0,4},{2,6},{4,8},{6,10},{8,12},{10,14},{12,16},{14,18},{16,20},{1... | collective-permute-start | bytes 786440 | tf_op jit(solution)/shard_map/ppermute | solution.py:12
  22.3 16.9 %collective-permute-start = (bf16[256,512]{1,0:T(8,128)(2,1)S(1)}, bf16[256,512]{1,0:T(8,128)(2,1)}, u32[]{:S(2)}, u32[]{:S(2)}) collective-permute-start(bf16[256,512]{1,0:T(8,128)(2,1)S(1)} %get-tuple-element.38), channel_id=1, source_target_pairs={{0,2},{2,4},{4,6},{6,8},{8,10},{10,12},{12,14},{14,16},{16,18},{18... | collective-permute-start | bytes 786440 | tf_op jit(solution)/shard_map/ppermute | solution.py:12
  24.2 16.0 %collective-permute-start.4 = (bf16[256,512]{1,0:T(8,128)(2,1)S(1)}, bf16[256,512]{1,0:T(8,128)(2,1)S(1)}, u32[]{:S(2)}, u32[]{:S(2)}) collective-permute-start(bf16[256,512]{1,0:T(8,128)(2,1)S(1)} %get-tuple-element.38), channel_id=1, source_target_pairs={{0,10},{2,12},{4,14},{6,16},{8,18},{10,20},{12,22},{14,24},{16,26}... | collective-permute-start | bytes 786440 | tf_op jit(solution)/shard_map/ppermute | solution.py:12
  45.5 25.9 %collective-permute-start.5 = (bf16[256,512]{0,1:T(8,128)(2,1)S(1)}, bf16[256,512]{0,1:T(8,128)(2,1)S(1)}, u32[]{:S(2)}, u32[]{:S(2)}) collective-permute-start(bf16[256,512]{0,1:T(8,128)(2,1)S(1)} %bitcast.268), channel_id=1, source_target_pairs={{0,2},{2,4},{4,6},{6,8},{8,10},{10,12},{12,14},{14,16},{16,18},{18... | collective-permute-start | bytes 786440 | tf_op jit(solution)/shard_map/ppermute | solution.py:12
  57.0 15.1 %collective-permute-start.6 = (bf16[256,512]{0,1:T(8,128)(2,1)S(1)}, bf16[256,512]{0,1:T(8,128)(2,1)S(1)}, u32[]{:S(2)}, u32[]{:S(2)}) collective-permute-start(bf16[256,512]{0,1:T(8,128)(2,1)S(1)} %bitcast.269), channel_id=1, source_target_pairs={{0,4},{2,6},{4,8},{6,10},{8,12},{10,14},{12,16},{14,18},{16,20},{1... | collective-permute-start | bytes 786440 | tf_op jit(solution)/shard_map/ppermute | solution.py:12
  59.0 15.4 %collective-permute-start.7 = (bf16[256,512]{0,1:T(8,128)(2,1)S(1)}, bf16[256,512]{0,1:T(8,128)(2,1)S(1)}, u32[]{:S(2)}, u32[]{:S(2)}) collective-permute-start(bf16[256,512]{0,1:T(8,128)(2,1)S(1)} %bitcast.270), channel_id=1, source_target_pairs={{0,6},{2,8},{4,10},{6,12},{8,14},{10,16},{12,18},{14,20},{16,22},{... | collective-permute-start | bytes 786440 | tf_op jit(solution)/shard_map/ppermute | solution.py:12
  67.5 17.4 %collective-permute-start.9 = (bf16[256,512]{0,1:T(8,128)(2,1)S(1)}, bf16[256,512]{0,1:T(8,128)(2,1)S(1)}, u32[]{:S(2)}, u32[]{:S(2)}) collective-permute-start(bf16[256,512]{0,1:T(8,128)(2,1)S(1)} %bitcast.271), channel_id=1, source_target_pairs={{0,10},{2,12},{4,14},{6,16},{8,18},{10,20},{12,22},{14,24},{16,26}... | collective-permute-start | bytes 786440 | tf_op jit(solution)/shard_map/ppermute | solution.py:12
  69.4 14.8 %collective-permute-start.8 = (bf16[256,512]{0,1:T(8,128)(2,1)S(1)}, bf16[256,512]{0,1:T(8,128)(2,1)S(1)}, u32[]{:S(2)}, u32[]{:S(2)}) collective-permute-start(bf16[256,512]{0,1:T(8,128)(2,1)S(1)} %bitcast.272), channel_id=1, source_target_pairs={{0,8},{2,10},{4,12},{6,14},{8,16},{10,18},{12,20},{14,22},{16,24},... | collective-permute-start | bytes 786440 | tf_op jit(solution)/shard_map/ppermute | solution.py:12
  92.2 19.7 %collective-permute-start.10 = (bf16[256,512]{0,1:T(8,128)(2,1)S(1)}, bf16[256,512]{0,1:T(8,128)(2,1)S(1)}, u32[]{:S(2)}, u32[]{:S(2)}) collective-permute-start(bf16[256,512]{0,1:T(8,128)(2,1)S(1)} %bitcast.273), channel_id=1, source_target_pairs={{0,2},{2,4},{4,6},{6,8},{8,10},{10,12},{12,14},{14,16},{16,18},{18... | collective-permute-start | bytes 786440 | tf_op jit(solution)/shard_map/ppermute | solution.py:12
  100.3 12.3 %collective-permute-start.11 = (bf16[256,512]{0,1:T(8,128)(2,1)S(1)}, bf16[256,512]{0,1:T(8,128)(2,1)S(1)}, u32[]{:S(2)}, u32[]{:S(2)}) collective-permute-start(bf16[256,512]{0,1:T(8,128)(2,1)S(1)} %bitcast.274), channel_id=1, source_target_pairs={{0,4},{2,6},{4,8},{6,10},{8,12},{10,14},{12,16},{14,18},{16,20},{1... | collective-permute-start | bytes 786440 | tf_op jit(solution)/shard_map/ppermute | solution.py:12
  102.3 14.3 %collective-permute-start.12 = (bf16[256,512]{0,1:T(8,128)(2,1)S(1)}, bf16[256,512]{0,1:T(8,128)(2,1)S(1)}, u32[]{:S(2)}, u32[]{:S(2)}) collective-permute-start(bf16[256,512]{0,1:T(8,128)(2,1)S(1)} %bitcast.275), channel_id=1, source_target_pairs={{0,6},{2,8},{4,10},{6,12},{8,14},{10,16},{12,18},{14,20},{16,22},{... | collective-permute-start | bytes 786440 | tf_op jit(solution)/shard_map/ppermute | solution.py:12
  107.6 18.9 %collective-permute-start.14 = (bf16[256,512]{0,1:T(8,128)(2,1)S(1)}, bf16[256,512]{0,1:T(8,128)(2,1)S(1)}, u32[]{:S(2)}, u32[]{:S(2)}) collective-permute-start(bf16[256,512]{0,1:T(8,128)(2,1)S(1)} %bitcast.276), channel_id=1, source_target_pairs={{0,10},{2,12},{4,14},{6,16},{8,18},{10,20},{12,22},{14,24},{16,26}... | collective-permute-start | bytes 786440 | tf_op jit(solution)/shard_map/ppermute | solution.py:12
  110.0 15.8 %collective-permute-start.13 = (bf16[256,512]{0,1:T(8,128)(2,1)S(1)}, bf16[256,512]{0,1:T(8,128)(2,1)S(1)}, u32[]{:S(2)}, u32[]{:S(2)}) collective-permute-start(bf16[256,512]{0,1:T(8,128)(2,1)S(1)} %bitcast.277), channel_id=1, source_target_pairs={{0,8},{2,10},{4,12},{6,14},{8,16},{10,18},{12,20},{14,22},{16,24},... | collective-permute-start | bytes 786440 | tf_op jit(solution)/shard_map/ppermute | solution.py:12
  146.5 21.4 %collective-permute-start.15 = (bf16[256,512]{0,1:T(8,128)(2,1)S(1)}, bf16[256,512]{0,1:T(8,128)(2,1)S(1)}, u32[]{:S(2)}, u32[]{:S(2)}) collective-permute-start(bf16[256,512]{0,1:T(8,128)(2,1)S(1)} %get-tuple-element.22), channel_id=1, source_target_pairs={{2,0},{4,2},{6,4},{8,6},{10,8},{12,10},{14,12},{16,14},{18,16},{20... | collective-permute-start | bytes 786440 | tf_op jit(solution)/shard_map/ppermute | solution.py:12
  148.4 19.5 %collective-permute-start.19 = (bf16[256,512]{0,1:T(8,128)(2,1)S(1)}, bf16[256,512]{0,1:T(8,128)(2,1)S(1)}, u32[]{:S(2)}, u32[]{:S(2)}) collective-permute-start(bf16[256,512]{0,1:T(8,128)(2,1)S(1)} %get-tuple-element.23), channel_id=1, source_target_pairs={{10,0},{12,2},{14,4},{16,6},{18,8},{20,10},{22,12},{24,14},{26,16}... | collective-permute-start | bytes 786440 | tf_op jit(solution)/shard_map/ppermute | solution.py:12
  150.3 17.6 %collective-permute-start.18 = (bf16[256,512]{0,1:T(8,128)(2,1)S(1)}, bf16[256,512]{0,1:T(8,128)(2,1)S(1)}, u32[]{:S(2)}, u32[]{:S(2)}) collective-permute-start(bf16[256,512]{0,1:T(8,128)(2,1)S(1)} %get-tuple-element.24), channel_id=1, source_target_pairs={{8,0},{10,2},{12,4},{14,6},{16,8},{18,10},{20,12},{22,14},{24,16},... | collective-permute-start | bytes 786440 | tf_op jit(solution)/shard_map/ppermute | solution.py:12
  152.3 15.6 %collective-permute-start.17 = (bf16[256,512]{0,1:T(8,128)(2,1)S(1)}, bf16[256,512]{0,1:T(8,128)(2,1)S(1)}, u32[]{:S(2)}, u32[]{:S(2)}) collective-permute-start(bf16[256,512]{0,1:T(8,128)(2,1)S(1)} %get-tuple-element.25), channel_id=1, source_target_pairs={{6,0},{8,2},{10,4},{12,6},{14,8},{16,10},{18,12},{20,14},{22,16},{... | collective-permute-start | bytes 786440 | tf_op jit(solution)/shard_map/ppermute | solution.py:12
  154.2 37.1 %collective-permute-start.16 = (bf16[256,512]{0,1:T(8,128)(2,1)S(1)}, bf16[256,512]{0,1:T(8,128)(2,1)S(1)}, u32[]{:S(2)}, u32[]{:S(2)}) collective-permute-start(bf16[256,512]{0,1:T(8,128)(2,1)S(1)} %get-tuple-element.26), channel_id=1, source_target_pairs={{4,0},{6,2},{8,4},{10,6},{12,8},{14,10},{16,12},{18,14},{20,16},{2... | collective-permute-start | bytes 786440 | tf_op jit(solution)/shard_map/ppermute | solution.py:12
  206.0 16.0 %collective-permute-start.20 = (bf16[256,512]{0,1:T(8,128)(2,1)S(1)}, bf16[256,512]{0,1:T(8,128)(2,1)S(1)}, u32[]{:S(2)}, u32[]{:S(2)}) collective-permute-start(bf16[256,512]{0,1:T(8,128)(2,1)S(1)} %get-tuple-element.17), channel_id=1, source_target_pairs={{2,0},{4,2},{6,4},{8,6},{10,8},{12,10},{14,12},{16,14},{18,16},{20... | collective-permute-start | bytes 786440 | tf_op jit(solution)/shard_map/ppermute | solution.py:12
  207.9 14.1 %collective-permute-start.24 = (bf16[256,512]{0,1:T(8,128)(2,1)S(1)}, bf16[256,512]{0,1:T(8,128)(2,1)S(1)}, u32[]{:S(2)}, u32[]{:S(2)}) collective-permute-start(bf16[256,512]{0,1:T(8,128)(2,1)S(1)} %get-tuple-element.18), channel_id=1, source_target_pairs={{10,0},{12,2},{14,4},{16,6},{18,8},{20,10},{22,12},{24,14},{26,16}... | collective-permute-start | bytes 786440 | tf_op jit(solution)/shard_map/ppermute | solution.py:12
  209.8 12.2 %collective-permute-start.23 = (bf16[256,512]{0,1:T(8,128)(2,1)S(1)}, bf16[256,512]{0,1:T(8,128)(2,1)S(1)}, u32[]{:S(2)}, u32[]{:S(2)}) collective-permute-start(bf16[256,512]{0,1:T(8,128)(2,1)S(1)} %get-tuple-element.19), channel_id=1, source_target_pairs={{8,0},{10,2},{12,4},{14,6},{16,8},{18,10},{20,12},{22,14},{24,16},... | collective-permute-start | bytes 786440 | tf_op jit(solution)/shard_map/ppermute | solution.py:12
  211.8 17.0 %collective-permute-start.22 = (bf16[256,512]{0,1:T(8,128)(2,1)S(1)}, bf16[256,512]{0,1:T(8,128)(2,1)S(1)}, u32[]{:S(2)}, u32[]{:S(2)}) collective-permute-start(bf16[256,512]{0,1:T(8,128)(2,1)S(1)} %get-tuple-element.20), channel_id=1, source_target_pairs={{6,0},{8,2},{10,4},{12,6},{14,8},{16,10},{18,12},{20,14},{22,16},{... | collective-permute-start | bytes 786440 | tf_op jit(solution)/shard_map/ppermute | solution.py:12
  213.7 25.9 %collective-permute-start.21 = (bf16[256,512]{0,1:T(8,128)(2,1)S(1)}, bf16[256,512]{0,1:T(8,128)(2,1)S(1)}, u32[]{:S(2)}, u32[]{:S(2)}) collective-permute-start(bf16[256,512]{0,1:T(8,128)(2,1)S(1)} %get-tuple-element.21), channel_id=1, source_target_pairs={{4,0},{6,2},{8,4},{10,6},{12,8},{14,10},{16,12},{18,14},{20,16},{2... | collective-permute-start | bytes 786440 | tf_op jit(solution)/shard_map/ppermute | solution.py:12
  251.8 15.2 %collective-permute-start.25 = (bf16[256,512]{1,0:T(8,128)(2,1)S(1)}, bf16[256,512]{1,0:T(8,128)(2,1)S(1)}, u32[]{:S(2)}, u32[]{:S(2)}) collective-permute-start(bf16[256,512]{1,0:T(8,128)(2,1)S(1)} %get-tuple-element.12), channel_id=1, source_target_pairs={{2,0},{4,2},{6,4},{8,6},{10,8},{12,10},{14,12},{16,14},{18,16},{20... | collective-permute-start | bytes 786440 | tf_op jit(solution)/shard_map/ppermute | solution.py:12
  253.9 13.2 %collective-permute-start.29 = (bf16[256,512]{1,0:T(8,128)(2,1)S(1)}, bf16[256,512]{1,0:T(8,128)(2,1)S(1)}, u32[]{:S(2)}, u32[]{:S(2)}) collective-permute-start(bf16[256,512]{1,0:T(8,128)(2,1)S(1)} %get-tuple-element.13), channel_id=1, source_target_pairs={{10,0},{12,2},{14,4},{16,6},{18,8},{20,10},{22,12},{24,14},{26,16}... | collective-permute-start | bytes 786440 | tf_op jit(solution)/shard_map/ppermute | solution.py:12
  255.8 12.4 %collective-permute-start.28 = (bf16[256,512]{1,0:T(8,128)(2,1)S(1)}, bf16[256,512]{1,0:T(8,128)(2,1)S(1)}, u32[]{:S(2)}, u32[]{:S(2)}) collective-permute-start(bf16[256,512]{1,0:T(8,128)(2,1)S(1)} %get-tuple-element.14), channel_id=1, source_target_pairs={{8,0},{10,2},{12,4},{14,6},{16,8},{18,10},{20,12},{22,14},{24,16},... | collective-permute-start | bytes 786440 | tf_op jit(solution)/shard_map/ppermute | solution.py:12
  257.7 16.3 %collective-permute-start.27 = (bf16[256,512]{1,0:T(8,128)(2,1)S(1)}, bf16[256,512]{1,0:T(8,128)(2,1)S(1)}, u32[]{:S(2)}, u32[]{:S(2)}) collective-permute-start(bf16[256,512]{1,0:T(8,128)(2,1)S(1)} %get-tuple-element.15), channel_id=1, source_target_pairs={{6,0},{8,2},{10,4},{12,6},{14,8},{16,10},{18,12},{20,14},{22,16},{... | collective-permute-start | bytes 786440 | tf_op jit(solution)/shard_map/ppermute | solution.py:12
  259.6 25.3 %collective-permute-start.26 = (bf16[256,512]{1,0:T(8,128)(2,1)S(1)}, bf16[256,512]{1,0:T(8,128)(2,1)S(1)}, u32[]{:S(2)}, u32[]{:S(2)}) collective-permute-start(bf16[256,512]{1,0:T(8,128)(2,1)S(1)} %get-tuple-element.16), channel_id=1, source_target_pairs={{4,0},{6,2},{8,4},{10,6},{12,8},{14,10},{16,12},{18,14},{20,16},{2... | collective-permute-start | bytes 786440 | tf_op jit(solution)/shard_map/ppermute | solution.py:12
  (12 other events, 318.4 us)
Sparse Core Ops, SparseCore 0:
  8.9 12.3 all-gather.1
where the time goes:
time: 296 us; the launch traced here: 295 us
  waiting for transfers between devices  118 us (40%)
  starting transfers between devices  90 us (30%)
  local copies, waits for them, and re-layouts  37.6 us (13%)
  matrix products  32.3 us (11%)
  between operations  14 us (5%)
    ppermute x30, waiting for transfers between devices, shifted(): return lax.ppermute(block, axis, route)  117 us
    ppermute x30, starting transfers between devices, shifted(): return lax.ppermute(block, axis, route)  90 us
    dot_general x3, matrix products, backward_parts(): jnp.einsum('ok,kac->oac', hits.astype(jnp.float32), terms, precision=lax....  12.7 us
    dot_general x3, local copies, waits for them, and re-layouts, backward_parts(): jnp.einsum('kba,bc->kac', blk, upper, preferred_element_type=jnp.float32)  10.3 us
    gather x3, local copies, waits for them, and re-layouts, forward_sums(): jnp.take(stacked, offset, axis=0)  8.46 us
    unnamed x38, local copies, waits for them, and re-layouts  7.46 us
    dot_general x2, matrix products, on_device(): jnp.dot(diag_all[level, 0], residue, preferred_element_type=jnp.float32)  6.41 us
  transfers between devices with their start and end apart: 31, of which 14 were waited for; matrix products, arithmetic and copies ran while one was open for 3% of the time, Pallas kernels for 0%

commit v1 on v0

v1 whole, which is shorter than its diff:
```python
import functools

import jax
import jax.numpy as jnp
from jax import lax
from jax.experimental import pallas as pl
from jax.experimental.pallas import tpu as pltpu
from jax.sharding import PartitionSpec as P

REACH = 5
GROUP = 4
F32 = jnp.float32
BF16 = jnp.bfloat16


def mm(a, b):
    return jnp.dot(a, b, preferred_element_type=F32)


def kernel(
    owners, ncores, nbr, rhs, blocks, diag, out,
    fac, win, rloc, solved_t, samp_t, near, far, stage, ostage,
    s_own, r_own, s_dg, r_dg, s_core, r_core, s_rhs, r_rhs, s_loc,
    s_x, r_x, s_b, r_b, s_o, r_o,
):
    levels = rhs.shape[0]
    rows = diag.shape[2]
    width = rhs.shape[3] // GROUP
    planes = owners // GROUP
    me = lax.axis_index("sweep")
    c = lax.axis_index("cols")
    k = me // GROUP
    i = me % GROUP
    px = i + 1 - 2 * (i % 2)
    py = (i + 2) % GROUP
    dg = GROUP - 1 - i
    base = k * GROUP
    peers = (px, py, dg)

    def at(owner, core):
        return (owner, core)

    def remote(src, dst, ssem, rsem, dev):
        return pltpu.make_async_remote_copy(
            src_ref=src, dst_ref=dst, send_sem=ssem, recv_sem=rsem,
            device_id=dev, device_id_type=pl.DeviceIdType.MESH,
        )

    win[:, 0:REACH] = jnp.zeros((levels - 1, REACH) + win.shape[2:], BF16)
    near[...] = jnp.zeros_like(near)
    far[...] = jnp.zeros_like(far)

    barrier = pltpu.get_barrier_semaphore()

    def greet(owner, core):
        pl.semaphore_signal(
            barrier, inc=1, device_id=at(owner, core), device_id_type=pl.DeviceIdType.MESH
        )

    for q in peers:
        greet(base + q, c)
    for r in range(1, ncores):
        greet(me, (c + r) % ncores)
    count = 3 + ncores - 1
    for d in (1, 2):
        @pl.when(k >= d)
        def _():
            greet(me - d * GROUP, c)

        @pl.when(k + d < planes)
        def _():
            greet(me + d * GROUP, c)

        count = count + jnp.where(k >= d, 1, 0) + jnp.where(k + d < planes, 1, 0)

    mine = pl.ds(pl.multiple_of(c * rows, rows), rows)
    for t in range(levels):
        fac[t, i, REACH + 1, mine, :] = diag[t, 0]
    for l in range(levels - 1):
        for o in range(REACH + 1):
            slot, hit = jnp.int32(0), jnp.int32(0)
            for s in range(blocks.shape[2]):
                got = nbr[l, s]
                same = (got == l * owners + me - o) & (got >= 0)
                slot = jnp.where(same, s, slot)
                hit = jnp.where(same, 1, hit)
            block = blocks[l, 0, slot].astype(F32) * hit.astype(F32)
            fac[l + 1, i, o, mine, :] = block.astype(BF16)

    pl.semaphore_wait(barrier, count)

    half = rows // 2

    def shard(t, owner):
        first = REACH + 1 if t == 0 else 0
        return fac.at[t, owner, pl.ds(first, REACH + 2 - first), mine, :]

    def shard_half(t, owner, h):
        first = REACH + 1 if t == 0 else 0
        part = pl.ds(pl.multiple_of(c * rows + h * half, half), half)
        return fac.at[t, owner, pl.ds(first, REACH + 2 - first), part, :]

    def own_copy(t, n):
        ref = shard(t, i)
        return remote(ref, ref, s_own.at[t, n], r_own.at[t, n], at(base + peers[n], c))

    def diag_copy(t, n):
        ref = shard_half(t, peers[n], n)
        return remote(ref, ref, s_dg.at[t, n], r_dg.at[t, n], at(base + peers[1 - n], c))

    def core_copy(t, source, r):
        ref = shard(t, ((i,) + peers)[source])
        return remote(
            ref, ref, s_core.at[t, source, r - 1], r_core.at[t, source, r - 1],
            at(me, (c + r) % ncores),
        )

    def rhs_copy(t, n):
        q = peers[n]
        cols = pl.ds(pl.multiple_of(q * width, width), width)
        return remote(
            rhs.at[t, 0, :, cols], rloc.at[t, i], s_rhs.at[t, n], r_rhs.at[t, n], at(base + q, c)
        )

    def rhs_local(t):
        cols = pl.ds(pl.multiple_of(i * width, width), width)
        return pltpu.make_async_copy(rhs.at[t, 0, :, cols], rloc.at[t, i], s_loc.at[t])

    cores = range(1, ncores)

    def start(t):
        for n in range(3):
            rhs_copy(t, n).start()
        rhs_local(t).start()
        for n in range(2):
            own_copy(t, n).start()
        for r in cores:
            core_copy(t, 0, r).start()

    def forward(t):
        for n in range(2):
            own_copy(t, n).wait_recv()
            diag_copy(t, n).start()
            for r in cores:
                core_copy(t, 1 + n, r).start()

    def finish_diag(t):
        for n in range(2):
            diag_copy(t, n).wait_recv()
        for r in cores:
            core_copy(t, 3, r).start()

    def arrived(t):
        for n in range(3):
            rhs_copy(t, n).wait_recv()
        rhs_local(t).wait()
        for source in range(4):
            for r in cores:
                core_copy(t, source, r).wait_recv()

    def sent(t):
        for n in range(3):
            rhs_copy(t, n).wait_send()
        for n in range(2):
            own_copy(t, n).wait_send()
            diag_copy(t, n).wait_send()
        for source in range(4):
            for r in cores:
                core_copy(t, source, r).wait_send()

    def solved_copy(l, n):
        j = GROUP - 1 if n == GROUP else n
        step, spot = (2, 0) if n == GROUP else (1, 1 + n)
        return remote(
            win.at[l, REACH + j], win.at[l, spot], s_x.at[l, n], r_x.at[l, n],
            at(me + step * GROUP, c),
        )

    def solve(l):
        for j in reversed(range(GROUP)):
            res = rloc[l, j]
            if l > 0:
                acc = mm(fac[l, j, 0], win[l - 1, REACH + j])
                for o in range(1, REACH + 1):
                    acc = acc + mm(fac[l, j, o], win[l - 1, REACH + j - o])
                res = (res.astype(F32) - acc).astype(BF16)
            y = mm(fac[l, j, REACH + 1], res)
            if l < levels - 1:
                win[l, REACH + j] = y.astype(BF16)

                @pl.when(k + 1 < planes)
                def _():
                    solved_copy(l, j).start()

                if j == GROUP - 1:
                    @pl.when(k + 2 < planes)
                    def _():
                        solved_copy(l, GROUP).start()

            solved_t[l, j] = y.T.astype(BF16)

    def solved_recv(l):
        @pl.when(k >= 1)
        def _():
            for n in range(GROUP):
                solved_copy(l, n).wait_recv()

        @pl.when(k >= 2)
        def _():
            solved_copy(l, GROUP).wait_recv()

    start(0)
    start(1)
    forward(0)
    if levels > 2:
        start(2)
    finish_diag(0)
    for l in range(levels):
        if l + 1 < levels:
            forward(l + 1)
        if l + 3 < levels:
            start(l + 3)
        arrived(l)
        if l > 0:
            solved_recv(l - 1)
        solve(l)
        if l + 1 < levels:
            finish_diag(l + 1)

    def term_copy(l, n):
        step, dst = (2, far.at[l]) if n == 0 else (1, near.at[l, n - 1])
        return remote(
            stage.at[l, n], dst, s_b.at[l, n], r_b.at[l, n], at(me - step * GROUP, c)
        )

    def out_copy(l, n):
        q = peers[n]
        cols = pl.ds(pl.multiple_of(i * width, width), width)
        return remote(
            ostage.at[l, q], out.at[l, 0, :, cols], s_o.at[l, n], r_o.at[l, n], at(base + q, c)
        )

    def out_local(l):
        cols = pl.ds(pl.multiple_of(i * width, width), width)
        return pltpu.make_async_copy(ostage.at[l, i], out.at[l, 0, :, cols], s_o.at[l, 3])

    def finish_level(l, adjusted):
        for j in range(GROUP):
            samp_t[l, j] = mm(adjusted[j], fac[l, j, REACH + 1]).astype(BF16)

    def emit(l):
        for j in range(GROUP):
            ostage[l, j] = samp_t[l, j].astype(F32).T.astype(BF16)
        for n in range(3):
            out_copy(l, n).start()
        out_local(l).start()

    def terms(l, w):
        total = None
        for j in range(max(0, w - REACH), min(GROUP - 1, w) + 1):
            term = mm(samp_t[l + 1, j], fac[l + 1, j, REACH + j - w])
            total = term if total is None else total + term
        return total

    top = levels - 1
    finish_level(top, [solved_t[top, j] for j in range(GROUP)])
    for l in range(levels - 2, -1, -1):
        for w in range(REACH):
            stage[l, w] = terms(l, w).astype(BF16)
            step = 2 if w == 0 else 1

            @pl.when(k >= step)
            def _():
                term_copy(l, w).start()

        emit(l + 1)
        back = [terms(l, REACH + j) for j in range(GROUP)]

        @pl.when(k + 1 < planes)
        def _():
            for n in range(1, REACH):
                term_copy(l, n).wait_recv()

        @pl.when(k + 2 < planes)
        def _():
            term_copy(l, 0).wait_recv()

        adjusted = []
        for j in range(GROUP):
            total = back[j] + near[l, j].astype(F32)
            if j == GROUP - 1:
                total = total + far[l].astype(F32)
            adjusted.append((solved_t[l, j].astype(F32) - total).astype(BF16))
        finish_level(l, adjusted)
    emit(0)

    for t in range(levels):
        sent(t)
    for l in range(levels - 1):
        @pl.when(k + 1 < planes)
        def _():
            for n in range(GROUP):
                solved_copy(l, n).wait_send()

        @pl.when(k + 2 < planes)
        def _():
            solved_copy(l, GROUP).wait_send()

        @pl.when(k >= 1)
        def _():
            for n in range(1, REACH):
                term_copy(l, n).wait_send()

        @pl.when(k >= 2)
        def _():
            term_copy(l, 0).wait_send()

    for l in range(levels):
        for n in range(3):
            out_copy(l, n).wait()
        out_local(l).wait()


def on_device(rhs, blocks, diag_inv, neighbours):
    owners = lax.axis_size("sweep")
    ncores = lax.axis_size("cols")
    levels, _, bs, cols = rhs.shape
    width = cols // GROUP
    dma = pltpu.SemaphoreType.DMA
    vmem = pl.BlockSpec(memory_space=pltpu.VMEM)
    return pl.pallas_call(
        functools.partial(kernel, owners, ncores),
        out_shape=jax.ShapeDtypeStruct(rhs.shape, rhs.dtype),
        in_specs=[pl.BlockSpec(memory_space=pltpu.SMEM), vmem, vmem, vmem],
        out_specs=vmem,
        scratch_shapes=[
            pltpu.VMEM((levels, GROUP, REACH + 2, bs, bs), BF16),
            pltpu.VMEM((levels - 1, REACH + GROUP, bs, width), BF16),
            pltpu.VMEM((levels, GROUP, bs, width), BF16),
            pltpu.VMEM((levels, GROUP, width, bs), BF16),
            pltpu.VMEM((levels, GROUP, width, bs), BF16),
            pltpu.VMEM((levels - 1, GROUP, width, bs), BF16),
            pltpu.VMEM((levels - 1, width, bs), BF16),
            pltpu.VMEM((levels - 1, REACH, width, bs), BF16),
            pltpu.VMEM((levels, GROUP, bs, width), BF16),
            dma((levels, 2)), dma((levels, 2)),
            dma((levels, 2)), dma((levels, 2)),
            dma((levels, 4, ncores - 1)), dma((levels, 4, ncores - 1)),
            dma((levels, 3)), dma((levels, 3)), dma((levels,)),
            dma((levels - 1, REACH)), dma((levels - 1, REACH)),
            dma((levels - 1, REACH)), dma((levels - 1, REACH)),
            dma((levels, 4)), dma((levels, 3)),
        ],
        compiler_params=pltpu.CompilerParams(
            collective_id=0, has_side_effects=True, vmem_limit_bytes=48 << 20
        ),
    )(neighbours[:, 0], rhs, blocks, diag_inv)


def solution(mesh):
    placed = (
        P(None, "sweep", None, "cols"),
        P(None, "sweep", None, "cols", None),
        P(None, "sweep", "cols", None),
        P(None, "sweep", None),
    )
    return jax.shard_map(
        on_device,
        mesh=mesh,
        in_specs=placed,
        out_specs=P(None, "sweep", None, "cols"),
        check_vma=False,
    )
```

time: 296 us -> 112 us (0.38)
  the two profiles are of different devices: /device:TPU:12 before, /device:TPU:0 now
where the time goes in v1:
time: 112 us
  Pallas kernels  107 us (96%)
  local copies, waits for them, and re-layouts  5.1 us (5%)
    pallas_call x1, Pallas kernels, on_device(): pl.pallas_call(functools.partial(kernel, owners, ncores), out_shape=jax.S...  107 us
    unnamed x8, local copies, waits for them, and re-layouts  5.1 us

profile of v1, /device:TPU:0, one launch (start us, length us, event | category | flops | bytes accessed | tf_op | source)
XLA Modules:
  0.0 112.3 jit_solution(8491115357649077822)
XLA Ops:
  0.0 0.7 copy.7
  0.7 0.0 copy-start
  0.7 1.3 %copy-done = bf16[3,1,6,128,256]{4,3,2,1,0:T(8,128)(2,1)S(1)} copy-done((bf16[3,1,6,128,256]{4,3,2,1,0:T(8,128)(2,1)S(1)}, bf16[3,1,6,128,256]{4,3,2,1,0:T(8,128)(2,1)}, u32[]{:S(2)}) %copy-start) | copy-done | bytes 1179672
  2.0 0.0 copy-start.1
  2.0 1.2 %copy-done.1 = bf16[4,1,256,512]{3,2,1,0:T(8,128)(2,1)S(1)} copy-done((bf16[4,1,256,512]{3,2,1,0:T(8,128)(2,1)S(1)}, bf16[4,1,256,512]{3,2,1,0:T(8,128)(2,1)}, u32[]{:S(2)}) %copy-start.1) | copy-done | bytes 1048600
  3.2 0.0 copy-start.2
  3.2 0.9 copy-done.2
  4.1 107.2 %shard_map.46 = bf16[4,1,256,512]{3,2,1,0:T(8,128)(2,1)S(1)} custom-call(s32[3,6]{1,0:T(4,128)S(1)} %bitcast.3, bf16[4,1,256,512]{3,2,1,0:T(8,128)(2,1)S(1)} %copy-done.1, bf16[3,1,6,128,256]{4,3,2,1,0:T(8,128)(2,1)S(1)} %copy-done, bf16[4,1,128,256]{3,2,1,0:T(8,128)(2,1)S(1)} %copy-done.2), custom_call_target="tpu_custom_call" | custom-call | tf_op jit(solution)/shard_map/pallas_call | solution.py:331
  111.3 1.0 copy.9
Async XLA Ops:
  0.7 1.3 %copy-start = (bf16[3,1,6,128,256]{4,3,2,1,0:T(8,128)(2,1)S(1)}, bf16[3,1,6,128,256]{4,3,2,1,0:T(8,128)(2,1)}, u32[]{:S(2)}) copy-start(bf16[3,1,6,128,256]{4,3,2,1,0:T(8,128)(2,1)} %blocks.1) | copy-start | bytes 3538948
  2.0 1.2 %copy-start.1 = (bf16[4,1,256,512]{3,2,1,0:T(8,128)(2,1)S(1)}, bf16[4,1,256,512]{3,2,1,0:T(8,128)(2,1)}, u32[]{:S(2)}) copy-start(bf16[4,1,256,512]{3,2,1,0:T(8,128)(2,1)} %rhs.1) | copy-start | bytes 3145732
  3.2 0.9 copy-start.2
